TPU v7x, 32 devices: a whole 2x2x4 slice. The times are simulated.
32 devices in a mesh: wide: 8 (over z, y), lev: 4 (over x, core).
Axes of the slice: x: 2, y: 2, z: 4, core: 2. Of those that a mesh axis runs over, the one named last changes fastest.
Arguments:
- state_field: float32 [12, 1472, 1472], P('lev', 'wide'), may hold values from -8 to 8
- to_modes: float32 [12, 12], replicated, may hold values from -4 to 4
- from_modes: float32 [12, 12], replicated, may hold values from -4 to 4, as said below
- mode_depth: float32 [12], replicated, may hold values from 0.1 to 2000
Outputs:
- updated_field: float32 [12, 1472, 1472], P('lev', 'wide')
Inputs may be any that keep to these rules, and one draw needn't show every extreme that they name: `from_modes`: the inverse of to_modes.
All inputs are finite; a program needn't handle non-finite values.
Results may differ from a plain program's by a relative error of at most 0.000094.
Values sent between devices are 32-bit elements; how exact they have to be, the bound alone decides.
No kernel may reach another device: no remote copies, remote signals or barrier semaphores. Data moves between devices by JAX's collectives and lax.ppermute only.
A program may use at most 64 MiB of HBM per device.

v0:
```python
import math
import jax
import jax.numpy as jnp
from jax import lax
from jax.sharding import PartitionSpec as P

I = 1472
E = 64
KT = 512
highest = lax.Precision.HIGHEST


def spread(block, axis, owner):
    block = jnp.where(lax.axis_index(axis) == owner, block, jnp.zeros_like(block))
    return lax.psum(block, axis)


def blend_weights(fraction):
    square = fraction * fraction
    cubed = square * fraction
    return (
        2.0 * cubed - 3.0 * square + 1.0,
        cubed - 2.0 * square + fraction,
        -2.0 * cubed + 3.0 * square,
        cubed - square,
    )


def hermite_mix(start_val, start_slope, end_val, end_slope, weights):
    return (
        weights[0] * end_val
        + weights[1] * end_slope
        + weights[2] * start_val
        + weights[3] * start_slope
    )


def extend_cols(sub_block, extra):
    fraction = (jnp.arange(extra, dtype=jnp.float32) + 1.0) / (extra + 1.0)
    weights = blend_weights(fraction)
    end_val = sub_block[..., -1:]
    end_slope = sub_block[..., -1:] - sub_block[..., -2:-1]
    start_val = sub_block[..., :1]
    start_slope = sub_block[..., 1:2] - sub_block[..., :1]
    added = hermite_mix(start_val, start_slope, end_val, end_slope, weights)
    return jnp.concatenate([sub_block, added], axis=-1)


def laplace(waves, length):
    sines = jnp.sin(math.pi / length * waves.astype(jnp.float32))
    return 4.0 * sines * sines


def cas_table(positions, waves, length):
    product = positions[:, None] * waves[None, :] % length
    phase_angle = 2.0 * math.pi / length * product.astype(jnp.float32)
    return jnp.cos(phase_angle) + jnp.sin(phase_angle)


def wave_numbers(amount, length, bound):
    indices = jnp.arange(amount, dtype=jnp.int32)
    waves = jnp.where(indices < bound, indices, length - 2 * bound + 1 + indices)
    live_mask = indices < 2 * bound - 1
    waves = jnp.where(live_mask, waves, 0)
    magnitude = jnp.minimum(waves, length - waves)
    return (waves, live_mask.astype(jnp.float32), magnitude)


def shards(state_field, to_modes, from_modes, mode_depth):
    wide_count = lax.axis_size("wide")
    wide_index = lax.axis_index("wide")
    lev_index = lax.axis_index("lev")
    levels, row_count, col_count = state_field.shape
    length = I + E
    ext_count = E // wide_count
    row_total = row_count + ext_count
    head_strip = spread(state_field[:, :2], "wide", 0)
    tail_strip = spread(state_field[:, row_count - 2 :], "wide", wide_count - 1)
    ext_slot = (wide_count - wide_index) % wide_count
    row_ids = ext_slot * ext_count + jnp.arange(ext_count, dtype=jnp.int32)
    fraction = (row_ids.astype(jnp.float32) + 1.0) / (E + 1.0)
    weights = tuple((weight[:, None] for weight in blend_weights(fraction)))
    end_val = tail_strip[:, 1:2]
    end_slope = tail_strip[:, 1:2] - tail_strip[:, 0:1]
    start_val = head_strip[:, 0:1]
    start_slope = head_strip[:, 1:2] - head_strip[:, 0:1]
    ext_block = hermite_mix(start_val, start_slope, end_val, end_slope, weights)
    stacked = jnp.concatenate([state_field, ext_block], axis=1)
    widened = extend_cols(stacked, E)
    spec_count = 2 * KT
    waves, live_mask, magnitude = wave_numbers(spec_count, length, KT)
    lap_all = laplace(waves, length)
    positions = jnp.arange(length, dtype=jnp.int32)
    forward_x = cas_table(positions, waves, length) * live_mask[None, :]
    row_owner = positions // row_total
    local_row = positions % row_total
    ext_owner = (wide_count - row_owner) % wide_count
    row_pos = jnp.where(
        local_row < row_count,
        row_owner * row_count + local_row,
        I + ext_owner * ext_count + local_row - row_count,
    )
    forward_y = cas_table(row_pos, waves, length) * live_mask[None, :]
    inverse_y = forward_y.T / length
    inverse_x = forward_x[:I].T / length
    col_span = spec_count // wide_count
    col_start = wide_index * col_span
    spec_x = jnp.einsum("irn,nc->irc", widened, forward_x, precision=highest)
    spectrum = jnp.einsum(
        "irc,rk->ick",
        lax.all_to_all(spec_x, "wide", split_axis=2, concat_axis=1, tiled=True),
        forward_y,
        precision=highest,
    )
    lev_start = lev_index * levels
    sub_block = lax.dynamic_slice(to_modes, (0, lev_start), (lax.axis_size("lev") * levels, levels))
    mode_values = lax.psum_scatter(
        jnp.einsum("ml,lck->mck", sub_block, spectrum, precision=highest),
        "lev",
        scatter_dimension=0,
        tiled=True,
    )
    lap_cols = lax.dynamic_slice_in_dim(lap_all, col_start, col_span)
    mag_cols = lax.dynamic_slice_in_dim(magnitude, col_start, col_span)
    live_cols = lax.dynamic_slice_in_dim(live_mask, col_start, col_span)
    inside = (
        mag_cols[:, None] * mag_cols[:, None] + magnitude[None, :] * magnitude[None, :] < KT * KT
    )
    keep_mask = live_cols[:, None] * live_mask[None, :] * inside.astype(jnp.float32)
    keep_mask, lap_sum = (keep_mask, lap_cols[:, None] + lap_all[None, :])
    mode_rates = lax.dynamic_slice_in_dim(mode_depth, lev_start, levels)
    solved = mode_values * keep_mask / (1.0 + mode_rates[:, None, None] * lap_sum)
    shard_piece = lax.all_gather(solved, "lev", axis=0, tiled=True)
    sub_block = lax.dynamic_slice(from_modes, (lev_start, 0), (levels, shard_piece.shape[0]))
    mixed_levels = jnp.einsum("lm,mck->lck", sub_block, shard_piece, precision=highest)
    rows_back = jnp.einsum("ick,kr->icr", mixed_levels, inverse_y, precision=highest)
    return jnp.einsum(
        "icr,cn->irn",
        lax.all_to_all(rows_back, "wide", split_axis=2, concat_axis=1, tiled=True)[
            :, :, :row_count
        ],
        inverse_x,
        precision=highest,
    )


def solution(mesh):
    placed = (P("lev", "wide", None), P(), P(), P())
    return jax.shard_map(
        shards, mesh=mesh, in_specs=placed, out_specs=P("lev", "wide", None), check_vma=False
    )
```

profile of v0, /device:TPU:0, one launch (start us, length us, event | category | flops | bytes accessed | tf_op | source)
XLA Modules:
  0.0 513.1 jit_solution(13678874333688489325)
XLA Ops:
  6.5 0.0 copy-start
  6.5 0.0 all-reduce.3.cloned.1.call-start
  6.5 1.8 slice_select_fusion.1
  8.3 0.0 all-reduce.3.cloned.1.call-update
  8.5 74.6 %all-reduce.3.cloned.1.call-done = (f32[3,2,1472]{2,1,0:T(2,128)}, f32[3,2,1472]{2,1,0:T(2,128)}) async-done(((f32[3,2,1472]{2,1,0:T(2,128)}, f32[3,2,1472]{2,1,0:T(2,128)}), (f32[3,2,1472]{2,1,0:T(2,128)}, f32[3,2,1472]{2,1,0:T(2,128)})) %all-reduce.3.cloned.1.call-update) | async-done | bytes 70672 | tf_op jit(solution)/shard_map/psum | solution.py:15
  83.1 0.9 fusion.107
  84.1 0.1 multiply_add_fusion.1
  84.2 2.0 fusion.66
  86.2 0.4 multiply_add_fusion
  86.6 0.0 copy-done.4
  86.6 0.4 fusion.124
  87.0 38.5 %fusion.12 = f32[3,192,1024]{2,1,0:T(8,128)S(1)} fusion(f32[1024]{0:T(1024)S(1)} %fusion.85, s32[1024]{0:T(1024)S(1)} %fusion.86, f32[3,192,1536]{2,1,0:T(8,128)S(1)} %fusion.124), kind=kOutput, calls=%fused_computation.15 | convolution fusion | flops 10888937472 | bytes 5906432 | tf_op jit(solution)/shard_map/irn,nc->irc/dot_general | solution.py:108
  125.5 3.2 copy.32
  128.7 4.8 all-to-all-start
  133.5 0.0 reduce-scatter.2.cloned.1.call-start
  133.5 91.4 %all-to-all-done = f32[3,192,1024]{1,0,2:T(4,128)} async-done(((f32[3,192,1024]{1,0,2:T(4,128)}), f32[3,192,1024]{1,0,2:T(4,128)}, u32[]{:S(2)}, u32[]{:S(2)}) %all-to-all-start) | async-done | bytes 2359328 | tf_op jit(solution)/shard_map/all_to_all | solution.py:111
  224.9 3.4 copy.45
  228.3 41.6 %fusion.10 = f32[3,128,1024]{2,1,0:T(8,128)S(1)} fusion(f32[3,1536,128]{2,1,0:T(8,128)S(1)} %bitcast.57, s32[1536]{0:T(1024)S(1)} %fusion.78, f32[1024]{0:T(1024)S(1)} %fusion.85, s32[1024]{0:T(1024)S(1)} %fusion.86), kind=kOutput, calls=%fused_computation.13 | convolution fusion | flops 7265058816 | bytes 3946496 | tf_op jit(solution)/shard_map/irc,rk->ick/dot_general | solution.py:109
  270.0 0.0 copy-done
  270.0 7.3 %fusion.59 = f32[12,128,1024]{2,0,1:T(8,128)S(1)} fusion(f32[3,128,1024]{2,1,0:T(8,128)S(1)} %fusion.10, f32[12,12]{1,0:T(8,128)S(1)} %copy-done, s32[]{:T(128)S(6)} %select_n.144), kind=kOutput, calls=%fused_computation.63 | convolution fusion | flops 56623104 | bytes 7864900 | tf_op jit(solution)/shard_map/ml,lck->mck/dot_general | solution.py:118
  277.3 6.3 %copy.37 = f32[12,128,1024]{2,1,0:T(8,128)} copy(f32[12,128,1024]{2,0,1:T(8,128)S(1)} %fusion.59) | data formatting | bytes 12582912 | tf_op jit(solution)/shard_map/ml,lck->mck/dot_general | solution.py:118
  283.6 0.0 reduce-scatter.2.cloned.1.call-update
  283.6 0.0 all-gather.2.cloned.1.call-start
  283.7 0.1 dynamic_slice.21
  283.8 0.1 dynamic_slice.23
  283.9 0.4 copy-done.5
  284.3 0.1 dynamic_slice.22
  284.3 0.1 dynamic-slice_multiply_fusion
  284.4 0.1 broadcast_add_fusion
  284.5 0.2 multiply_select_fusion
  284.7 56.9 %reduce-scatter.2.cloned.1.call-done = f32[3,128,1024]{2,1,0:T(8,128)} async-done(((f32[12,128,1024]{2,1,0:T(8,128)}), f32[3,128,1024]{2,1,0:T(8,128)}) %reduce-scatter.2.cloned.1.call-update) | async-done | bytes 1572880 | tf_op jit(solution)/shard_map/reduce_scatter | solution.py:117
  341.7 2.9 add_divide_fusion
  344.6 0.0 all-gather.2.cloned.1.call-update
  344.7 27.9 %fusion.122 = f32[1024,1536,1]{1,0,2:T(8,128)} fusion(f32[1024]{0:T(1024)S(1)} %fusion.85, s32[1024]{0:T(1024)S(1)} %fusion.86, s32[1536]{0:T(1024)S(1)} %fusion.78), kind=kLoop, calls=%fused_computation.12.clone.1 | loop fusion | flops 18874368 | bytes 6305792 | tf_op jit(solution)/shard_map/ick,kr->icr/dot_general | solution.py:136
  372.5 18.7 %all-gather.2.cloned.1.call-done = f32[12,128,1024]{2,1,0:T(8,128)} async-done(((f32[3,128,1024]{2,1,0:T(8,128)}), f32[12,128,1024]{2,1,0:T(8,128)}) %all-gather.2.cloned.1.call-update) | async-done | bytes 6291472 | tf_op jit(solution)/shard_map/all_gather | solution.py:133
  391.2 11.3 %fusion = f32[3,128,1024]{2,0,1:T(4,128)S(1)} fusion(f32[12,128,1024]{2,1,0:T(8,128)} %all-gather.2.cloned.1.call-done, f32[12,12]{1,0:T(8,128)} %param.6, s32[]{:T(128)S(6)} %select_n.144), kind=kOutput, calls=%fused_computation.3 | convolution fusion | flops 56623104 | bytes 7866372 | tf_op jit(solution)/shard_map/lm,mck->lck/dot_general | solution.py:135
  402.5 0.0 copy-done.2
  402.5 8.6 %fusion.8 = f32[3,128,1536]{2,1,0:T(8,128)S(1)} fusion(f32[3,128,1024]{2,0,1:T(4,128)S(1)} %fusion, f32[1024,1536,1]{1,0,2:T(8,128)S(1)} %copy-done.2), kind=kOutput, calls=%fused_computation.11 | convolution fusion | flops 7247757312 | bytes 10223616 | tf_op jit(solution)/shard_map/ick,kr->icr/dot_general | solution.py:136
  411.1 2.7 copy.40
  413.9 5.8 %all-to-all-start.1 = ((f32[3,128,1536]{1,0,2:T(4,128)}), f32[3,128,1536]{1,0,2:T(4,128)S(1)}, u32[]{:S(2)}, u32[]{:S(2)}) async-start(f32[3,128,1536]{1,0,2:T(4,128)} %copy.40), calls=%async_computation.2 | async-start | bytes 6291456 | tf_op jit(solution)/shard_map/all_to_all | solution.py:139
  419.6 27.2 %add_multiply_fusion = f32[1536,1024]{1,0:T(8,128)} fusion(f32[1024]{0:T(1024)S(1)} %fusion.85, s32[1024]{0:T(1024)S(1)} %fusion.86), kind=kLoop, calls=%fused_computation.32 | loop fusion | flops 17301504 | bytes 6299648 | tf_op jit(solution)/shard_map/mul | solution.py:94
  446.8 43.9 %all-to-all-done.1 = f32[3,128,1536]{1,0,2:T(4,128)S(1)} async-done(((f32[3,128,1536]{1,0,2:T(4,128)}), f32[3,128,1536]{1,0,2:T(4,128)S(1)}, u32[]{:S(2)}, u32[]{:S(2)}) %all-to-all-start.1) | async-done | bytes 2359328 | tf_op jit(solution)/shard_map/all_to_all | solution.py:139
  490.7 0.2 copy.41
  490.9 0.0 copy-start.1
  490.9 0.3 copy.64
  491.2 2.3 copy-done.3
  493.5 12.7 %fusion.37 = f32[3,184,1472]{2,1,0:T(8,128)} fusion(f32[1536,1024]{1,0:T(8,128)S(1)} %copy-done.3, f32[3,1024,192]{1,2,0:T(8,128)S(1)} %bitcast.56), kind=kOutput, calls=%fused_computation.41 | convolution fusion | flops 9986048000 | bytes 11540480 | tf_op jit(solution)/shard_map/icr,cn->irn/dot_general | solution.py:137
  506.2 0.0 copy-done.1
  (18 shorter events, 0.2 us)
Async XLA Ops:
  6.5 263.4 %copy-start = (f32[12,12]{1,0:T(8,128)S(1)}, f32[12,12]{1,0:T(8,128)}, u32[]{:S(2)}) copy-start(f32[12,12]{1,0:T(8,128)} %param.5) | copy-start | bytes 1732
  6.5 80.1 %copy-start.4 = (f32[3,184,1472]{2,1,0:T(8,128)S(1)}, f32[3,184,1472]{2,1,0:T(8,128)}, u32[]{:S(2)}) copy-start(f32[3,184,1472]{2,1,0:T(8,128)} %param.4) | copy-start | bytes 9750532
  6.5 76.5 %all-reduce.3.cloned.1.call-start = ((), (), s32[]{:S(2)}) async-start(), calls=%async_computation.5 | async-start | bytes 147456 | tf_op jit(solution)/shard_map/psum | solution.py:15
  128.7 96.2 %all-to-all-start = ((f32[3,192,1024]{1,0,2:T(4,128)}), f32[3,192,1024]{1,0,2:T(4,128)}, u32[]{:S(2)}, u32[]{:S(2)}) async-start(f32[3,192,1024]{1,0,2:T(4,128)} %copy.32), calls=%async_computation | async-start | bytes 8388608 | tf_op jit(solution)/shard_map/all_to_all | solution.py:111
  133.5 208.2 %reduce-scatter.2.cloned.1.call-start = ((), (), s32[]{:S(2)}) async-start(), calls=%async_computation.3 | async-start | bytes 7864320 | tf_op jit(solution)/shard_map/reduce_scatter | solution.py:117
  283.6 0.7 copy-start.5
  283.6 107.5 %all-gather.2.cloned.1.call-start = ((), (), s32[]{:S(2)}) async-start(), calls=%async_computation.4 | async-start | bytes 7864320 | tf_op jit(solution)/shard_map/all_gather | solution.py:133
  391.2 11.4 %copy-start.2 = (f32[1024,1536,1]{1,0,2:T(8,128)S(1)}, f32[1024,1536,1]{1,0,2:T(8,128)}, u32[]{:S(2)}) copy-start(f32[1024,1536,1]{1,0,2:T(8,128)} %fusion.122) | copy-start | bytes 18874372
  413.9 76.8 %all-to-all-start.1 = ((f32[3,128,1536]{1,0,2:T(4,128)}), f32[3,128,1536]{1,0,2:T(4,128)S(1)}, u32[]{:S(2)}, u32[]{:S(2)}) async-start(f32[3,128,1536]{1,0,2:T(4,128)} %copy.40), calls=%async_computation.2 | async-start | bytes 6291456 | tf_op jit(solution)/shard_map/all_to_all | solution.py:139
  490.7 2.8 copy-start.3
  490.9 15.3 %copy-start.1 = (f32[12,12]{1,0:T(8,128)S(1)}, f32[12,12]{1,0:T(8,128)}, u32[]{:S(2)}) copy-start(f32[12,12]{1,0:T(8,128)} %param.5) | copy-start | bytes 1732
Sparse Core Ops, SparseCore 0:
  10.8 72.1 all-reduce.2
  283.8 57.8 reduce-scatter.1
  344.8 46.3 all-gather.1
where the time goes:
time: 522 us; the launch traced here: 513 us
  waiting for transfers between devices  286 us (55%)
  matrix products  120 us (23%)
  other arithmetic  64.1 us (12%)
  local copies, waits for them, and re-layouts  19 us (4%)
  between operations  13.7 us (3%)
  starting transfers between devices  10.6 us (2%)
    all_to_all x1, waiting for transfers between devices, shards(): lax.all_to_all(spec_x, 'wide', split_axis=2, concat_axis=1, tiled=True)  91.4 us
    psum x1, waiting for transfers between devices, spread(): return lax.psum(block, axis)  74.6 us
    reduce_scatter x1, waiting for transfers between devices, shards(): lax.psum_scatter(jnp.einsum('ml,lck->mck', sub_block, spectrum, precision...  56.9 us
    all_to_all x1, waiting for transfers between devices, shards(): lax.all_to_all(rows_back, 'wide', split_axis=2, concat_axis=1, tiled=True)  43.9 us
    dot_general x1, matrix products, shards(): jnp.einsum('irc,rk->ick', lax.all_to_all(spec_x, 'wide', split_axis=2, co...  41.6 us
    dot_general x1, matrix products, shards(): spec_x = jnp.einsum('irn,nc->irc', widened, forward_x, precision=highest)  38.5 us
    dot_general x1, other arithmetic, shards(): jnp.einsum('ick,kr->icr', mixed_levels, inverse_y, precision=highest)  27.9 us
    mul x1, other arithmetic, shards(): forward_x = cas_table(positions, waves, length) * live_mask[None, :]  27.2 us
  transfers between devices with their start and end apart: 5, of which 5 were waited for; matrix products, arithmetic and copies ran while one was open for 11% of the time, Pallas kernels for 0%

commit v1 on v0

--- a/solution.py
+++ b/solution.py
@@ -108,7 +108,12 @@
     spec_x = jnp.einsum("irn,nc->irc", widened, forward_x, precision=highest)
     spectrum = jnp.einsum(
         "irc,rk->ick",
-        lax.all_to_all(spec_x, "wide", split_axis=2, concat_axis=1, tiled=True),
+        jnp.concatenate(
+            lax.all_to_all(
+                jnp.stack(jnp.split(spec_x, lax.axis_size("wide"), axis=2)), "wide", 0, 0
+            ),
+            axis=1,
+        ),
         forward_y,
         precision=highest,
     )

time: 522 us -> 483 us (0.925)
  waiting for transfers between devices: 286 us -> 246 us
    all_to_all x1, waiting for transfers between devices: 91.4 us -> 52 us  [shards(): lax.all_to_all(jnp.stack(jnp.split(spec_x, lax.axis_size('wide'), axis=2)...]
    unnamed x16 -> x23, local copies, waits for them, and re-layouts: 2.72 us -> 8 us
  transfers between devices with their start and end apart: 5 -> 5, of which waited for: 5 -> 5; matrix products, arithmetic and copies ran while one was open for 11% -> 12% of each run, Pallas kernels for 0% -> 0%
where the time goes in v1:
time: 483 us; the launch traced here: 473 us
  waiting for transfers between devices  246 us (51%)
  matrix products  120 us (25%)
  other arithmetic  64.1 us (13%)
  local copies, waits for them, and re-layouts  18.7 us (4%)
  between operations  13.7 us (3%)
  starting transfers between devices  10.4 us (2%)
    psum x1, waiting for transfers between devices, spread(): return lax.psum(block, axis)  74.6 us
    reduce_scatter x1, waiting for transfers between devices, shards(): lax.psum_scatter(jnp.einsum('ml,lck->mck', sub_block, spectrum, precision...  56.9 us
    all_to_all x1, waiting for transfers between devices, shards(): lax.all_to_all(jnp.stack(jnp.split(spec_x, lax.axis_size('wide'), axis=2)...  52 us
    all_to_all x1, waiting for transfers between devices, shards(): lax.all_to_all(rows_back, 'wide', split_axis=2, concat_axis=1, tiled=True)  43.9 us
    dot_general x1, matrix products, shards(): jnp.einsum('irc,rk->ick', jnp.concatenate(lax.all_to_all(jnp.stack(jnp.sp...  41.9 us
    dot_general x1, matrix products, shards(): spec_x = jnp.einsum('irn,nc->irc', widened, forward_x, precision=highest)  38.5 us
    dot_general x1, other arithmetic, shards(): jnp.einsum('ick,kr->icr', mixed_levels, inverse_y, precision=highest)  27.9 us
    mul x1, other arithmetic, shards(): forward_x = cas_table(positions, waves, length) * live_mask[None, :]  27.2 us
  transfers between devices with their start and end apart: 5, of which 5 were waited for; matrix products, arithmetic and copies ran while one was open for 12% of the time, Pallas kernels for 0%

profile of v1, /device:TPU:0, one launch (start us, length us, event | category | flops | bytes accessed | tf_op | source)
XLA Modules:
  0.0 473.3 jit_solution(4524985406859621668)
XLA Ops:
  6.5 1.8 slice_select_fusion.1
  8.3 0.0 all-reduce.3.cloned.1.call-update
  8.5 74.6 %all-reduce.3.cloned.1.call-done = (f32[3,2,1472]{2,1,0:T(2,128)}, f32[3,2,1472]{2,1,0:T(2,128)}) async-done(((f32[3,2,1472]{2,1,0:T(2,128)}, f32[3,2,1472]{2,1,0:T(2,128)}), (f32[3,2,1472]{2,1,0:T(2,128)}, f32[3,2,1472]{2,1,0:T(2,128)})) %all-reduce.3.cloned.1.call-update) | async-done | bytes 70672 | tf_op jit(solution)/shard_map/psum | solution.py:15
  83.1 0.9 fusion.115
  84.1 0.1 multiply_add_fusion.1
  84.2 2.0 fusion.74
  86.2 0.4 multiply_add_fusion
  86.6 0.4 fusion.132
  87.0 38.5 %fusion.12 = f32[3,192,1024]{2,1,0:T(8,128)S(1)} fusion(f32[1024]{0:T(1024)S(1)} %fusion.93, s32[1024]{0:T(1024)S(1)} %fusion.94, f32[3,192,1536]{2,1,0:T(8,128)S(1)} %fusion.132), kind=kOutput, calls=%fused_computation.15 | convolution fusion | flops 10888937472 | bytes 5906432 | tf_op jit(solution)/shard_map/irn,nc->irc/dot_general | solution.py:108
  125.5 0.8 fusion.69
  126.2 0.8 fusion.68
  127.0 0.8 fusion.67
  127.7 0.8 fusion.66
  128.5 0.8 fusion.65
  129.3 0.8 fusion.64
  130.0 0.8 fusion.63
  130.8 0.8 fusion.62
  131.5 4.6 all-to-all-start
  136.1 0.0 reduce-scatter.2.cloned.1.call-start
  136.2 52.0 %all-to-all-done = f32[8,3,192,128]{3,2,1,0:T(8,128)S(1)} async-done(((f32[8,3,192,128]{3,2,1,0:T(8,128)}), f32[8,3,192,128]{3,2,1,0:T(8,128)S(1)}, u32[]{:S(2)}, u32[]{:S(2)}) %all-to-all-start) | async-done | bytes 2359328 | tf_op jit(solution)/shard_map/all_to_all | solution.py:112
  188.1 0.2 copy.20
  188.3 41.9 %fusion.10 = f32[3,128,1024]{2,1,0:T(8,128)S(1)} fusion(f32[3,1536,128]{2,1,0:T(8,128)S(1)} %bitcast.87, s32[1536]{0:T(1024)S(1)} %fusion.86, f32[1024]{0:T(1024)S(1)} %fusion.93, s32[1024]{0:T(1024)S(1)} %fusion.94), kind=kOutput, calls=%fused_computation.13 | convolution fusion | flops 7265058816 | bytes 3946496 | tf_op jit(solution)/shard_map/irc,rk->ick/dot_general | solution.py:109
  230.3 7.3 %fusion.59 = f32[12,128,1024]{2,0,1:T(8,128)S(1)} fusion(f32[3,128,1024]{2,1,0:T(8,128)S(1)} %fusion.10, f32[12,12]{1,0:T(8,128)S(1)} %copy-done, s32[]{:T(128)S(6)} %select_n.144), kind=kOutput, calls=%fused_computation.63 | convolution fusion | flops 56623104 | bytes 7864900 | tf_op jit(solution)/shard_map/ml,lck->mck/dot_general | solution.py:123
  237.6 6.3 %copy.23 = f32[12,128,1024]{2,1,0:T(8,128)} copy(f32[12,128,1024]{2,0,1:T(8,128)S(1)} %fusion.59) | data formatting | bytes 12582912 | tf_op jit(solution)/shard_map/ml,lck->mck/dot_general | solution.py:123
  243.9 0.0 reduce-scatter.2.cloned.1.call-update
  243.9 0.0 all-gather.2.cloned.1.call-start
  244.0 0.1 dynamic_slice.21
  244.1 0.1 dynamic_slice.23
  244.2 0.4 copy-done.5
  244.6 0.1 dynamic_slice.22
  244.6 0.1 dynamic-slice_multiply_fusion
  244.7 0.1 broadcast_add_fusion
  244.8 0.2 multiply_select_fusion
  245.0 56.9 %reduce-scatter.2.cloned.1.call-done = f32[3,128,1024]{2,1,0:T(8,128)} async-done(((f32[12,128,1024]{2,1,0:T(8,128)}), f32[3,128,1024]{2,1,0:T(8,128)}) %reduce-scatter.2.cloned.1.call-update) | async-done | bytes 1572880 | tf_op jit(solution)/shard_map/reduce_scatter | solution.py:122
  301.9 2.9 add_divide_fusion
  304.9 0.0 all-gather.2.cloned.1.call-update
  304.9 27.9 %fusion.130 = f32[1024,1536,1]{1,0,2:T(8,128)} fusion(f32[1024]{0:T(1024)S(1)} %fusion.93, s32[1024]{0:T(1024)S(1)} %fusion.94, s32[1536]{0:T(1024)S(1)} %fusion.86), kind=kLoop, calls=%fused_computation.12.clone.1 | loop fusion | flops 18874368 | bytes 6305792 | tf_op jit(solution)/shard_map/ick,kr->icr/dot_general | solution.py:141
  332.8 18.7 %all-gather.2.cloned.1.call-done = f32[12,128,1024]{2,1,0:T(8,128)} async-done(((f32[3,128,1024]{2,1,0:T(8,128)}), f32[12,128,1024]{2,1,0:T(8,128)}) %all-gather.2.cloned.1.call-update) | async-done | bytes 6291472 | tf_op jit(solution)/shard_map/all_gather | solution.py:138
  351.4 11.3 %fusion = f32[3,128,1024]{2,0,1:T(4,128)S(1)} fusion(f32[12,128,1024]{2,1,0:T(8,128)} %all-gather.2.cloned.1.call-done, f32[12,12]{1,0:T(8,128)} %param.6, s32[]{:T(128)S(6)} %select_n.144), kind=kOutput, calls=%fused_computation.3 | convolution fusion | flops 56623104 | bytes 7866372 | tf_op jit(solution)/shard_map/lm,mck->lck/dot_general | solution.py:140
  362.8 8.6 %fusion.8 = f32[3,128,1536]{2,1,0:T(8,128)S(1)} fusion(f32[3,128,1024]{2,0,1:T(4,128)S(1)} %fusion, f32[1024,1536,1]{1,0,2:T(8,128)S(1)} %copy-done.2), kind=kOutput, calls=%fused_computation.11 | convolution fusion | flops 7247757312 | bytes 10223616 | tf_op jit(solution)/shard_map/ick,kr->icr/dot_general | solution.py:141
  371.4 2.7 copy.26
  374.1 5.8 %all-to-all-start.1 = ((f32[3,128,1536]{1,0,2:T(4,128)}), f32[3,128,1536]{1,0,2:T(4,128)S(1)}, u32[]{:S(2)}, u32[]{:S(2)}) async-start(f32[3,128,1536]{1,0,2:T(4,128)} %copy.26), calls=%async_computation.2 | async-start | bytes 6291456 | tf_op jit(solution)/shard_map/all_to_all | solution.py:144
  379.9 27.2 %add_multiply_fusion = f32[1536,1024]{1,0:T(8,128)} fusion(f32[1024]{0:T(1024)S(1)} %fusion.93, s32[1024]{0:T(1024)S(1)} %fusion.94), kind=kLoop, calls=%fused_computation.32 | loop fusion | flops 17301504 | bytes 6299648 | tf_op jit(solution)/shard_map/mul | solution.py:94
  407.1 43.9 %all-to-all-done.1 = f32[3,128,1536]{1,0,2:T(4,128)S(1)} async-done(((f32[3,128,1536]{1,0,2:T(4,128)}), f32[3,128,1536]{1,0,2:T(4,128)S(1)}, u32[]{:S(2)}, u32[]{:S(2)}) %all-to-all-start.1) | async-done | bytes 2359328 | tf_op jit(solution)/shard_map/all_to_all | solution.py:144
  451.0 0.2 copy.27
  451.1 0.3 copy.48
  451.4 2.3 copy-done.3
  453.7 12.7 %fusion.37 = f32[3,184,1472]{2,1,0:T(8,128)} fusion(f32[1536,1024]{1,0:T(8,128)S(1)} %copy-done.3, f32[3,1024,192]{1,2,0:T(8,128)S(1)} %bitcast.86), kind=kOutput, calls=%fused_computation.41 | convolution fusion | flops 9986048000 | bytes 11540480 | tf_op jit(solution)/shard_map/icr,cn->irn/dot_general | solution.py:142
  (25 shorter events, 0.2 us)
Async XLA Ops:
  6.5 223.7 %copy-start = (f32[12,12]{1,0:T(8,128)S(1)}, f32[12,12]{1,0:T(8,128)}, u32[]{:S(2)}) copy-start(f32[12,12]{1,0:T(8,128)} %param.5) | copy-start | bytes 1732
  6.5 80.1 %copy-start.4 = (f32[3,184,1472]{2,1,0:T(8,128)S(1)}, f32[3,184,1472]{2,1,0:T(8,128)}, u32[]{:S(2)}) copy-start(f32[3,184,1472]{2,1,0:T(8,128)} %param.4) | copy-start | bytes 9750532
  6.5 76.5 %all-reduce.3.cloned.1.call-start = ((), (), s32[]{:S(2)}) async-start(), calls=%async_computation.5 | async-start | bytes 147456 | tf_op jit(solution)/shard_map/psum | solution.py:15
  131.5 56.6 %all-to-all-start = ((f32[8,3,192,128]{3,2,1,0:T(8,128)}), f32[8,3,192,128]{3,2,1,0:T(8,128)S(1)}, u32[]{:S(2)}, u32[]{:S(2)}) async-start(f32[8,3,192,128]{3,2,1,0:T(8,128)} %fusion.62), calls=%async_computation | async-start | bytes 4718592 | tf_op jit(solution)/shard_map/all_to_all | solution.py:112
  136.1 165.8 %reduce-scatter.2.cloned.1.call-start = ((), (), s32[]{:S(2)}) async-start(), calls=%async_computation.3 | async-start | bytes 7864320 | tf_op jit(solution)/shard_map/reduce_scatter | solution.py:122
  243.9 0.7 copy-start.5
  243.9 107.5 %all-gather.2.cloned.1.call-start = ((), (), s32[]{:S(2)}) async-start(), calls=%async_computation.4 | async-start | bytes 7864320 | tf_op jit(solution)/shard_map/all_gather | solution.py:138
  351.4 11.4 %copy-start.2 = (f32[1024,1536,1]{1,0,2:T(8,128)S(1)}, f32[1024,1536,1]{1,0,2:T(8,128)}, u32[]{:S(2)}) copy-start(f32[1024,1536,1]{1,0,2:T(8,128)} %fusion.130) | copy-start | bytes 18874372
  374.1 76.8 %all-to-all-start.1 = ((f32[3,128,1536]{1,0,2:T(4,128)}), f32[3,128,1536]{1,0,2:T(4,128)S(1)}, u32[]{:S(2)}, u32[]{:S(2)}) async-start(f32[3,128,1536]{1,0,2:T(4,128)} %copy.26), calls=%async_computation.2 | async-start | bytes 6291456 | tf_op jit(solution)/shard_map/all_to_all | solution.py:144
  451.0 2.8 copy-start.3
  451.4 15.0 %copy-start.1 = (f32[12,12]{1,0:T(8,128)S(1)}, f32[12,12]{1,0:T(8,128)}, u32[]{:S(2)}) copy-start(f32[12,12]{1,0:T(8,128)} %param.5) | copy-start | bytes 1732
Sparse Core Ops, SparseCore 0:
  10.8 72.1 all-reduce.2
  244.1 57.8 reduce-scatter.1
  305.0 46.3 all-gather.1
